TPU v7x, 32 devices: a whole 2x2x4 slice. The times are simulated.
32 devices in a mesh: groups: 2 (over y), expert: 4 (over z), dp: 4 (over x, core).
Axes of the slice: x: 2, y: 2, z: 4, core: 2. Of those that a mesh axis runs over, the one named last changes fastest.
Arguments:
- tokens: bfloat16 [2048, 1024], P(('groups', 'expert', 'dp')), parts along dimension 0, may hold values from -6 to 6
- expert_ids: int32 [2048, 8], P(('groups', 'expert', 'dp')), parts along dimension 0, may hold values from 0 to 31, all different within a row; in each aligned block of 64 rows (0 to 63, 64 to 127, ...) at most 32 rows name the same one
- route_scores: float32 [2048, 8], P(('groups', 'expert', 'dp')), parts along dimension 0, may hold values from 0.05 to 1
- w_gate: bfloat16 [32, 1024, 768], P('expert'), may hold values from -0.1875 to 0.1875
- w_up: bfloat16 [32, 1024, 768], P('expert'), may hold values from -0.1875 to 0.1875
- w_down: bfloat16 [32, 768, 1024], P('expert'), may hold values from -0.21875 to 0.21875
Outputs:
- mixed: bfloat16 [2048, 1024], P(('groups', 'expert', 'dp')), parts along dimension 0
There are 2 independent parts, one for each index of `groups`. A program takes and returns all parts, laid end to end along the dimension named above; an argument that names none is the same for every part. Nothing has to cross between parts.
Inputs may be any that keep to these rules, and one draw needn't show every extreme that they name: `expert_ids`: within the 64 rows of one device no expert is named by more than 32 rows, and in every draw some expert is named by exactly 32 rows of some device.
All inputs are finite; a program needn't handle non-finite values.
Results may differ from a plain program's by a relative error of at most 0.0064.
Values may be sent and summed in bfloat16 or wider, within the bound.
No kernel may reach another device: no remote copies, remote signals or barrier semaphores. Data moves between devices by JAX's collectives and lax.ppermute only.
A program may use at most 128 MiB of HBM per device.

v0:
```python
import math
import jax
import jax.numpy as jnp
from jax import lax
from jax.sharding import PartitionSpec as P

EXPERTS = 32
TOP = 8
CAP = 32


def lookup(values, indices, length):
    match = indices[:, None] == jnp.arange(length, dtype=jnp.int32)[None, :]
    return jnp.sum(jnp.where(match, values[None, :], 0), axis=1)


def compact_plan(source_counts, peer_count):
    slot_span = peer_count * CAP
    source_ends = jnp.cumsum(source_counts)
    starts = source_ends - source_counts
    position = jnp.arange(slot_span, dtype=jnp.int32)
    source_of = jnp.minimum(
        jnp.sum((source_ends[None, :] <= position[:, None]).astype(jnp.int32), axis=1),
        peer_count - 1,
    )
    gather_at = jnp.clip(
        source_of * CAP + position - lookup(starts, source_of, peer_count), 0, slot_span - 1
    )
    live_rows = position < source_ends[peer_count - 1]
    return (gather_at, live_rows, starts)


def spread_back(compact_out, source_counts, starts, peer_count):
    slot_span = peer_count * CAP
    position = jnp.arange(slot_span, dtype=jnp.int32)
    source_of = position // CAP
    within = position % CAP
    from_pos = jnp.minimum(lookup(starts, source_of, peer_count) + within, slot_span - 1)
    live_slots = within < lookup(source_counts, source_of, peer_count)
    return jnp.where(live_slots[:, None], compact_out[from_pos], jnp.zeros((), jnp.bfloat16))


def expert_rows(row_block, scale_block, weight_set, row_count, tile_rows):
    gate_matrix, up_matrix, down_matrix = weight_set
    initial = jnp.zeros(row_block.shape, jnp.bfloat16)
    turn_count = (row_count + tile_rows - 1) // tile_rows

    def advance(loop_state):
        turn_index, filled = loop_state
        offset = turn_index * tile_rows
        part_rows = lax.dynamic_slice_in_dim(row_block, offset, tile_rows, 0)
        part_scale = lax.dynamic_slice_in_dim(scale_block, offset, tile_rows, 0)
        gate_values = jnp.dot(part_rows, gate_matrix, preferred_element_type=jnp.float32)
        up_values = jnp.dot(part_rows, up_matrix, preferred_element_type=jnp.float32)
        hidden = (jax.nn.silu(gate_values) * up_values).astype(jnp.bfloat16)
        projected = jnp.dot(hidden, down_matrix, preferred_element_type=jnp.float32)
        scaled = (part_scale.astype(jnp.float32)[:, None] * projected).astype(jnp.bfloat16)
        return (turn_index + 1, lax.dynamic_update_slice_in_dim(filled, scaled, offset, 0))

    def pending(loop_state):
        return loop_state[0] < turn_count

    return lax.while_loop(pending, advance, (jnp.int32(0), initial))[1]


def per_device(tokens, expert_ids, route_scores, w_gate, w_up, w_down):
    peer_count = lax.axis_size("expert")
    local_experts = w_gate.shape[0]
    token_count = tokens.shape[0]
    model_width = tokens.shape[1]
    slot_count = token_count * TOP
    slot_span = peer_count * CAP
    half_span = slot_span // 2
    tile_rows = math.gcd(half_span, 256)
    route_weights = (route_scores / jnp.sum(route_scores, axis=1, keepdims=True)).astype(
        jnp.bfloat16
    )
    flat_ids = expert_ids.reshape(slot_count)
    onehot = (flat_ids[:, None] == jnp.arange(EXPERTS, dtype=jnp.int32)[None, :]).astype(jnp.int32)
    slot_ranks = jnp.sum((jnp.cumsum(onehot, axis=0) - 1) * onehot, axis=1)
    targets = flat_ids * CAP + slot_ranks
    source_slot = (
        jnp.full((EXPERTS * CAP,), slot_count, jnp.int32)
        .at[targets]
        .set(jnp.arange(slot_count, dtype=jnp.int32))
    )
    padded_tokens = jnp.concatenate([tokens, jnp.zeros((1, model_width), jnp.bfloat16)], axis=0)
    padded_weights = jnp.concatenate(
        [route_weights.reshape(slot_count), jnp.zeros((1,), jnp.bfloat16)]
    )
    send_rows = padded_tokens[source_slot // TOP].reshape(EXPERTS, CAP, model_width)
    send_scale = padded_weights[source_slot].reshape(EXPERTS, CAP)
    recv_rows, recv_scale = (
        lax.all_to_all(send_rows, "expert", split_axis=0, concat_axis=1, tiled=True),
        lax.all_to_all(send_scale, "expert", split_axis=0, concat_axis=1, tiled=True),
    )
    compact_rows = []
    compact_scale = []
    count_list = []
    start_list = []
    total_list = []
    for member in range(local_experts):
        source_counts = jnp.sum(
            (recv_scale[member].reshape(peer_count, CAP) > 0).astype(jnp.int32), axis=1
        )
        gather_at, live_rows, starts = compact_plan(source_counts, peer_count)
        compact_rows.append(
            jnp.where(live_rows[:, None], recv_rows[member][gather_at], jnp.zeros((), jnp.bfloat16))
        )
        compact_scale.append(
            jnp.where(live_rows, recv_scale[member][gather_at], jnp.zeros((), jnp.bfloat16))
        )
        count_list.append(source_counts)
        start_list.append(starts)
        total_list.append(jnp.sum(source_counts))
    results = []
    for member in range(local_experts):
        results.append(
            expert_rows(
                compact_rows[member],
                compact_scale[member],
                (w_gate[member], w_up[member], w_down[member]),
                total_list[member],
                tile_rows,
            )
        )
    slot_results = jnp.stack(
        [
            spread_back(results[member], count_list[member], start_list[member], peer_count)
            for member in range(local_experts)
        ]
    )
    returned = lax.all_to_all(slot_results, "expert", split_axis=1, concat_axis=0, tiled=True)
    returned_flat = returned.reshape(EXPERTS * CAP, model_width)
    picked = returned_flat[targets].astype(jnp.float32).reshape(token_count, TOP, model_width)
    return jnp.sum(picked, axis=1).astype(jnp.bfloat16)


def solution(mesh):
    placed = (
        P(("groups", "expert", "dp"), None),
        P(("groups", "expert", "dp"), None),
        P(("groups", "expert", "dp"), None),
        P("expert", None, None),
        P("expert", None, None),
        P("expert", None, None),
    )
    return jax.shard_map(
        per_device,
        mesh=mesh,
        in_specs=placed,
        out_specs=P(("groups", "expert", "dp"), None),
        check_vma=False,
    )
```

profile of v0, /device:TPU:0, one launch (start us, length us, event | category | flops | bytes accessed | tf_op | source)
XLA Modules:
  0.0 296.0 jit_solution(2162845717473998222)
XLA Ops:
  5.0 2.4 scatter_custom_fusion
  7.5 6.8 %gather_fusion = bf16[1024]{0:T(1024)(128)(2,1)S(1)} fusion(bf16[513]{0:T(1024)(128)(2,1)S(1)} %pad_maximum_fusion, s32[1024]{0:T(1024)S(1)} %get-tuple-element.566), kind=kCustom, calls=%fused_computation | custom fusion | bytes 8192 | tf_op jit(solution)/shard_map/gather | solution.py:92
  15.1 6.3 %all-to-all-start = ((bf16[4,2,128]{2,1,0:T(2,128)(2,1)}), bf16[4,2,128]{2,1,0:T(2,128)(2,1)S(1)}, u32[]{:S(2)}, u32[]{:S(2)}) async-start(bf16[4,2,128]{2,1,0:T(2,128)(2,1)} %reshape.1325), calls=%async_computation | async-start | bytes 4096 | tf_op jit(solution)/shard_map/all_to_all | solution.py:95
  21.4 9.6 %slice_bitcast_fusion = (bf16[768,1024]{1,0:T(8,128)(2,1)}, bf16[768,1024]{1,0:T(8,128)(2,1)}, bf16[768,1024]{1,0:T(8,128)(2,1)}, bf16[768,1024]{1,0:T(8,128)(2,...) fusion(bf16[8,768,1024]{2,1,0:T(8,128)(2,1)} %param.27), kind=kLoop, calls=%fused_computation.173 | loop fusion | bytes 25165824 | tf_op jit(solution)/shard_map/squeeze | solution.py:122
  31.0 17.0 %slice_bitcast_fusion.1 = (bf16[1024,768]{1,0:T(8,128)(2,1)S(1)}, bf16[1024,768]{1,0:T(8,128)(2,1)}, bf16[1024,768]{1,0:T(8,128)(2,1)}, bf16[1024,768]{1,0:T(8,1...) fusion(bf16[8,1024,768]{2,1,0:T(8,128)(2,1)} %param.26, ...), kind=kLoop, calls=%fused_computation.174 | loop fusion | bytes 50331648 | tf_op jit(solution)/shard_map/squeeze | solution.py:122
  48.1 5.4 %gather_fusion.2 = bf16[1024,1024]{1,0:T(8,128)(2,1)} fusion(bf16[65,1024]{1,0:T(8,128)(2,1)S(1)} %concatenate.7, s32[1024]{0:T(1024)S(1)} %get-tuple-element.565), kind=kCustom, calls=%fused_computation.2 | custom fusion | bytes 4198400 | tf_op jit(solution)/shard_map/gather | solution.py:91
  53.5 5.1 %all-to-all-start.1 = ((bf16[32,32,1024]{2,1,0:T(8,128)(2,1)}), bf16[32,32,1024]{2,1,0:T(8,128)(2,1)}, u32[]{:S(2)}, u32[]{:S(2)}) async-start(bf16[32,32,1024]{2,1,0:T(8,128)(2,1)} %bitcast.390), calls=%async_computation.1 | async-start | bytes 4194304 | tf_op jit(solution)/shard_map/all_to_all | solution.py:94
  58.7 1.4 fusion.168
  96.4 9.9 %all-to-all-done.1 = bf16[32,32,1024]{2,1,0:T(8,128)(2,1)} async-done(((bf16[32,32,1024]{2,1,0:T(8,128)(2,1)}), bf16[32,32,1024]{2,1,0:T(8,128)(2,1)}, u32[]{:S(2)}, u32[]{:S(2)}) %all-to-all-start.1) | async-done | bytes 2097184 | tf_op jit(solution)/shard_map/all_to_all | solution.py:94
  106.3 1.8 copy.42
  109.4 2.7 gather_fusion.3
  112.1 1.7 broadcast_select_fusion.7
  114.6 12.2 %while.80 = (s32[]{:T(128)}, bf16[128,1024]{1,0:T(8,128)(2,1)}, s32[]{:T(128)}, bf16[128]{0:T(256)(128)(2,1)S(1)}, bf16[128,1024]{1,0:T(8,128)(2,1)}, /*index=5*...) while((s32[]{:T(128)}, bf16[128,1024]{1,0:T(8,128)(2,1)}, ...), condition=%wide.region_12.13_spmd, body=%wide.region_11.12_spmd.sunk | while | flops 302415936 | bytes 5506867 | solution.py:63
  114.6 2.6 fusion.295
  117.2 3.4 %fusion.296 = bf16[128,1024]{1,0:T(8,128)(2,1)} fusion(bf16[128,1024]{1,0:T(8,128)(2,1)} %get-tuple-element.989, s32[]{:T(128)S(6)} %select_n.860, bf16[768,1024]{1,0:T(8,128)(2,1)} %get-tuple-element.1007, bf16[1024,768]{1,0:T(8,128)(2,1)} %get-tuple-element.1006, f32[64,768]{1,0:T(8,128)} %fusion.295, f32[64]{0:T(128)S(1)} %dynamic-slice_convert_fusion.16, ...), kind=kOutput, calls=%fused_computation.31.clone.1 | convolution fusion | flops 201752576 | bytes 3605760 | tf_op jit(solution)/shard_map/while/body/dot_general | solution.py:56
  120.7 2.6 fusion.295
  123.3 3.4 %fusion.296 = bf16[128,1024]{1,0:T(8,128)(2,1)} fusion(bf16[128,1024]{1,0:T(8,128)(2,1)} %get-tuple-element.989, s32[]{:T(128)S(6)} %select_n.860, bf16[768,1024]{1,0:T(8,128)(2,1)} %get-tuple-element.1007, bf16[1024,768]{1,0:T(8,128)(2,1)} %get-tuple-element.1006, f32[64,768]{1,0:T(8,128)} %fusion.295, f32[64]{0:T(128)S(1)} %dynamic-slice_convert_fusion.16, ...), kind=kOutput, calls=%fused_computation.31.clone.1 | convolution fusion | flops 201752576 | bytes 3605760 | tf_op jit(solution)/shard_map/while/body/dot_general | solution.py:56
  126.8 2.7 gather_fusion.6
  129.5 1.7 broadcast_select_fusion.6
  132.0 6.1 %while.81 = (s32[]{:T(128)}, bf16[128,1024]{1,0:T(8,128)(2,1)}, s32[]{:T(128)}, bf16[128]{0:T(256)(128)(2,1)S(1)}, bf16[128,1024]{1,0:T(8,128)(2,1)}, /*index=5*...) while((s32[]{:T(128)}, bf16[128,1024]{1,0:T(8,128)(2,1)}, ...), condition=%wide.region_21.22_spmd, body=%wide.region_20.21_spmd.sunk | while | flops 302415936 | bytes 5506867 | solution.py:63
  132.0 2.6 fusion.302
  134.7 3.5 %fusion.303 = bf16[128,1024]{1,0:T(8,128)(2,1)} fusion(bf16[128,1024]{1,0:T(8,128)(2,1)} %get-tuple-element.1025, s32[]{:T(128)S(6)} %select_n.861, bf16[768,1024]{1,0:T(8,128)(2,1)} %get-tuple-element.1043, bf16[1024,768]{1,0:T(8,128)(2,1)} %get-tuple-element.1042, f32[64,768]{1,0:T(8,128)} %fusion.302, f32[64]{0:T(128)S(1)} %dynamic-slice_convert_fusion.17, ...), kind=kOutput, calls=%fused_computation.49.clone.1 | convolution fusion | flops 201752576 | bytes 3605760 | tf_op jit(solution)/shard_map/while/body/dot_general | solution.py:56
  138.1 2.7 gather_fusion.9
  140.8 1.8 broadcast_select_fusion.5
  143.3 6.1 %while.82 = (s32[]{:T(128)}, bf16[128,1024]{1,0:T(8,128)(2,1)}, s32[]{:T(128)}, bf16[128]{0:T(256)(128)(2,1)S(1)}, bf16[128,1024]{1,0:T(8,128)(2,1)}, /*index=5*...) while((s32[]{:T(128)}, bf16[128,1024]{1,0:T(8,128)(2,1)}, ...), condition=%wide.region_30.31_spmd, body=%wide.region_29.30_spmd.sunk | while | flops 302415936 | bytes 5506867 | solution.py:63
  143.3 2.6 fusion.309
  146.0 3.4 %fusion.310 = bf16[128,1024]{1,0:T(8,128)(2,1)} fusion(bf16[128,1024]{1,0:T(8,128)(2,1)} %get-tuple-element.1061, s32[]{:T(128)S(6)} %select_n.862, bf16[768,1024]{1,0:T(8,128)(2,1)} %get-tuple-element.1079, bf16[1024,768]{1,0:T(8,128)(2,1)} %get-tuple-element.1078, f32[64,768]{1,0:T(8,128)} %fusion.309, f32[64]{0:T(128)S(1)} %dynamic-slice_convert_fusion.18, ...), kind=kOutput, calls=%fused_computation.67.clone.1 | convolution fusion | flops 201752576 | bytes 3605760 | tf_op jit(solution)/shard_map/while/body/dot_general | solution.py:56
  149.4 2.7 gather_fusion.12
  152.2 1.8 broadcast_select_fusion.4
  154.6 12.1 %while.83 = (s32[]{:T(128)}, bf16[128,1024]{1,0:T(8,128)(2,1)}, s32[]{:T(128)}, bf16[128]{0:T(256)(128)(2,1)S(1)}, bf16[128,1024]{1,0:T(8,128)(2,1)}, /*index=5*...) while((s32[]{:T(128)}, bf16[128,1024]{1,0:T(8,128)(2,1)}, ...), condition=%wide.region_39.40_spmd, body=%wide.region_38.39_spmd.sunk | while | flops 302415936 | bytes 5506867 | solution.py:63
  154.6 2.5 fusion.316
  157.3 3.4 %fusion.317 = bf16[128,1024]{1,0:T(8,128)(2,1)} fusion(bf16[128,1024]{1,0:T(8,128)(2,1)} %get-tuple-element.1097, s32[]{:T(128)S(6)} %select_n.863, bf16[768,1024]{1,0:T(8,128)(2,1)} %get-tuple-element.1115, bf16[1024,768]{1,0:T(8,128)(2,1)} %get-tuple-element.1114, f32[64,768]{1,0:T(8,128)} %fusion.316, f32[64]{0:T(128)S(1)} %dynamic-slice_convert_fusion.19, ...), kind=kOutput, calls=%fused_computation.85.clone.1 | convolution fusion | flops 201752576 | bytes 3605760 | tf_op jit(solution)/shard_map/while/body/dot_general | solution.py:56
  160.7 2.5 fusion.316
  163.3 3.5 %fusion.317 = bf16[128,1024]{1,0:T(8,128)(2,1)} fusion(bf16[128,1024]{1,0:T(8,128)(2,1)} %get-tuple-element.1097, s32[]{:T(128)S(6)} %select_n.863, bf16[768,1024]{1,0:T(8,128)(2,1)} %get-tuple-element.1115, bf16[1024,768]{1,0:T(8,128)(2,1)} %get-tuple-element.1114, f32[64,768]{1,0:T(8,128)} %fusion.316, f32[64]{0:T(128)S(1)} %dynamic-slice_convert_fusion.19, ...), kind=kOutput, calls=%fused_computation.85.clone.1 | convolution fusion | flops 201752576 | bytes 3605760 | tf_op jit(solution)/shard_map/while/body/dot_general | solution.py:56
  166.8 2.7 gather_fusion.15
  169.5 1.8 broadcast_select_fusion.3
  172.0 6.1 %while.84 = (s32[]{:T(128)}, bf16[128,1024]{1,0:T(8,128)(2,1)}, s32[]{:T(128)}, bf16[128]{0:T(256)(128)(2,1)S(1)}, bf16[128,1024]{1,0:T(8,128)(2,1)}, /*index=5*...) while((s32[]{:T(128)}, bf16[128,1024]{1,0:T(8,128)(2,1)}, ...), condition=%wide.region_48.49_spmd, body=%wide.region_47.48_spmd.sunk | while | flops 302415936 | bytes 5506867 | solution.py:63
  172.0 2.5 fusion.323
  174.6 3.4 %fusion.324 = bf16[128,1024]{1,0:T(8,128)(2,1)} fusion(bf16[128,1024]{1,0:T(8,128)(2,1)} %get-tuple-element.1133, s32[]{:T(128)S(6)} %select_n.864, bf16[768,1024]{1,0:T(8,128)(2,1)} %get-tuple-element.1151, bf16[1024,768]{1,0:T(8,128)(2,1)} %get-tuple-element.1150, f32[64,768]{1,0:T(8,128)} %fusion.323, f32[64]{0:T(128)S(1)} %dynamic-slice_convert_fusion.20, ...), kind=kOutput, calls=%fused_computation.103.clone.1 | convolution fusion | flops 201752576 | bytes 3605760 | tf_op jit(solution)/shard_map/while/body/dot_general | solution.py:56
  178.1 2.7 gather_fusion.18
  180.8 1.7 broadcast_select_fusion.2
  183.3 12.2 %while.85 = (s32[]{:T(128)}, bf16[128,1024]{1,0:T(8,128)(2,1)}, s32[]{:T(128)}, bf16[128]{0:T(256)(128)(2,1)S(1)}, bf16[128,1024]{1,0:T(8,128)(2,1)}, /*index=5*...) while((s32[]{:T(128)}, bf16[128,1024]{1,0:T(8,128)(2,1)}, ...), condition=%wide.region_57.58_spmd, body=%wide.region_56.57_spmd.sunk | while | flops 302415936 | bytes 5506867 | solution.py:63
  183.3 2.6 fusion.330
  186.0 3.4 %fusion.331 = bf16[128,1024]{1,0:T(8,128)(2,1)} fusion(bf16[128,1024]{1,0:T(8,128)(2,1)} %get-tuple-element.1169, s32[]{:T(128)S(6)} %select_n.865, bf16[768,1024]{1,0:T(8,128)(2,1)} %get-tuple-element.1187, bf16[1024,768]{1,0:T(8,128)(2,1)} %get-tuple-element.1186, f32[64,768]{1,0:T(8,128)} %fusion.330, f32[64]{0:T(128)S(1)} %dynamic-slice_convert_fusion.21, ...), kind=kOutput, calls=%fused_computation.121.clone.1 | convolution fusion | flops 201752576 | bytes 3605760 | tf_op jit(solution)/shard_map/while/body/dot_general | solution.py:56
  189.4 2.6 fusion.330
  192.0 3.4 %fusion.331 = bf16[128,1024]{1,0:T(8,128)(2,1)} fusion(bf16[128,1024]{1,0:T(8,128)(2,1)} %get-tuple-element.1169, s32[]{:T(128)S(6)} %select_n.865, bf16[768,1024]{1,0:T(8,128)(2,1)} %get-tuple-element.1187, bf16[1024,768]{1,0:T(8,128)(2,1)} %get-tuple-element.1186, f32[64,768]{1,0:T(8,128)} %fusion.330, f32[64]{0:T(128)S(1)} %dynamic-slice_convert_fusion.21, ...), kind=kOutput, calls=%fused_computation.121.clone.1 | convolution fusion | flops 201752576 | bytes 3605760 | tf_op jit(solution)/shard_map/while/body/dot_general | solution.py:56
  195.5 2.7 gather_fusion.21
  198.2 1.7 broadcast_select_fusion.1
  200.7 11.4 %while.86 = (s32[]{:T(128)}, bf16[128,1024]{1,0:T(8,128)(2,1)}, s32[]{:T(128)}, bf16[128]{0:T(256)(128)(2,1)S(1)}, bf16[128,1024]{1,0:T(8,128)(2,1)}, /*index=5*...) while((s32[]{:T(128)}, bf16[128,1024]{1,0:T(8,128)(2,1)}, ...), condition=%wide.region_66.67_spmd, body=%wide.region_65.66_spmd.sunk | while | flops 302415936 | bytes 5506867 | solution.py:63
  200.7 2.6 fusion.337
  203.4 3.1 %fusion.338 = bf16[128,1024]{1,0:T(8,128)(2,1)} fusion(bf16[128,1024]{1,0:T(8,128)(2,1)} %get-tuple-element.1205, s32[]{:T(128)S(6)} %select_n.866, bf16[768,1024]{1,0:T(8,128)(2,1)} %get-tuple-element.1223, bf16[1024,768]{1,0:T(8,128)(2,1)S(1)} %get-tuple-element.1222, f32[64,768]{1,0:T(8,128)} %fusion.337, ...), kind=kOutput, calls=%fused_computation.139.clone.1 | convolution fusion | flops 201752576 | bytes 3605760 | tf_op jit(solution)/shard_map/while/body/dot_general | solution.py:56
  206.4 2.6 fusion.337
  209.1 3.1 %fusion.338 = bf16[128,1024]{1,0:T(8,128)(2,1)} fusion(bf16[128,1024]{1,0:T(8,128)(2,1)} %get-tuple-element.1205, s32[]{:T(128)S(6)} %select_n.866, bf16[768,1024]{1,0:T(8,128)(2,1)} %get-tuple-element.1223, bf16[1024,768]{1,0:T(8,128)(2,1)S(1)} %get-tuple-element.1222, f32[64,768]{1,0:T(8,128)} %fusion.337, ...), kind=kOutput, calls=%fused_computation.139.clone.1 | convolution fusion | flops 201752576 | bytes 3605760 | tf_op jit(solution)/shard_map/while/body/dot_general | solution.py:56
  212.1 1.6 gather_fusion.24
  213.7 1.7 broadcast_select_fusion
  215.5 9.2 %while.87 = (s32[]{:T(128)}, bf16[128,1024]{1,0:T(8,128)(2,1)S(1)}, s32[]{:T(128)}, bf16[128]{0:T(256)(128)(2,1)S(1)}, bf16[128,1024]{1,0:T(8,128)(2,1)}, /*inde...) while((s32[]{:T(128)}, bf16[128,1024]{1,0:T(8,128)(2,1)S(1)}, ...), condition=%wide.region_75.76_spmd, body=%wide.region_74.75_spmd.sunk | while | flops 302415936 | bytes 5507123 | solution.py:63
  215.5 2.0 fusion.344
  217.6 2.4 fusion.345
  220.0 2.0 fusion.344
  222.0 2.4 fusion.345
  224.7 2.1 gather_fusion.4
  239.6 2.7 copy.37
  242.4 49.1 %all_to_all.46 = bf16[8,128,1024]{2,0,1:T(8,128)(2,1)S(1)} all-to-all(bf16[8,128,1024]{2,0,1:T(8,128)(2,1)S(1)} %copy.37), channel_id=1, replica_groups=mesh['groups'=2,'expert'=4,'dp'=4] {'expert'}, dimensions={1} | all-to-all | bytes 4194304 | tf_op jit(solution)/shard_map/all_to_all | solution.py:133
  292.6 2.1 gather_fusion.26
  (206 shorter events, 59.2 us)
Async XLA Ops:
  15.1 38.4 %all-to-all-start = ((bf16[4,2,128]{2,1,0:T(2,128)(2,1)}), bf16[4,2,128]{2,1,0:T(2,128)(2,1)S(1)}, u32[]{:S(2)}, u32[]{:S(2)}) async-start(bf16[4,2,128]{2,1,0:T(2,128)(2,1)} %reshape.1325), calls=%async_computation | async-start | bytes 4096 | tf_op jit(solution)/shard_map/all_to_all | solution.py:95
  31.0 17.1 %copy-start.7 = (bf16[64,1024]{1,0:T(8,128)(2,1)S(1)}, bf16[64,1024]{1,0:T(8,128)(2,1)}, u32[]{:S(2)}) copy-start(bf16[64,1024]{1,0:T(8,128)(2,1)} %param.22) | copy-start | bytes 393220
  53.5 52.8 %all-to-all-start.1 = ((bf16[32,32,1024]{2,1,0:T(8,128)(2,1)}), bf16[32,32,1024]{2,1,0:T(8,128)(2,1)}, u32[]{:S(2)}, u32[]{:S(2)}) async-start(bf16[32,32,1024]{2,1,0:T(8,128)(2,1)} %bitcast.390), calls=%async_computation.1 | async-start | bytes 4194304 | tf_op jit(solution)/shard_map/all_to_all | solution.py:94
  126.8 5.2 %copy-start.12 = (bf16[128]{0:T(256)(128)(2,1)S(1)}, bf16[128]{0:T(256)(128)(2,1)}, u32[]{:S(2)}) copy-start(bf16[128]{0:T(256)(128)(2,1)} %broadcast_select_fusion.14) | copy-start | bytes 772
  138.1 5.2 %copy-start.11 = (bf16[128]{0:T(256)(128)(2,1)S(1)}, bf16[128]{0:T(256)(128)(2,1)}, u32[]{:S(2)}) copy-start(bf16[128]{0:T(256)(128)(2,1)} %broadcast_select_fusion.13) | copy-start | bytes 772
  149.4 5.2 %copy-start.10 = (bf16[128]{0:T(256)(128)(2,1)S(1)}, bf16[128]{0:T(256)(128)(2,1)}, u32[]{:S(2)}) copy-start(bf16[128]{0:T(256)(128)(2,1)} %broadcast_select_fusion.12) | copy-start | bytes 772
  166.8 5.2 %copy-start.9 = (bf16[128]{0:T(256)(128)(2,1)S(1)}, bf16[128]{0:T(256)(128)(2,1)}, u32[]{:S(2)}) copy-start(bf16[128]{0:T(256)(128)(2,1)} %broadcast_select_fusion.11) | copy-start | bytes 772
  178.1 5.2 %copy-start.8 = (bf16[128]{0:T(256)(128)(2,1)S(1)}, bf16[128]{0:T(256)(128)(2,1)}, u32[]{:S(2)}) copy-start(bf16[128]{0:T(256)(128)(2,1)} %broadcast_select_fusion.10) | copy-start | bytes 772
  212.1 3.4 %copy-start = (bf16[1024,768]{1,0:T(8,128)(2,1)S(1)}, bf16[1024,768]{1,0:T(8,128)(2,1)}, u32[]{:S(2)}) copy-start(bf16[1024,768]{1,0:T(8,128)(2,1)} %get-tuple-element.1233) | copy-start | bytes 4718596
  224.7 2.9 copy-start.1
  226.8 1.7 copy-start.2
  228.4 1.0 copy-start.3
  229.3 1.0 copy-start.4
  230.3 1.0 copy-start.5
  231.2 1.0 copy-start.6
where the time goes:
time: 298 us; the launch traced here: 296 us
  local copies, waits for them, and re-layouts  102 us (34%)
  matrix products  74 us (25%)
  blocking collectives  49.1 us (16%)
  other arithmetic  42.9 us (14%)
  starting transfers between devices  11.4 us (4%)
  waiting for transfers between devices  9.93 us (3%)
  between operations  5.99 us (2%)
    all_to_all x1, blocking collectives, per_device(): lax.all_to_all(slot_results, 'expert', split_axis=1, concat_axis=0, tiled...  49.1 us
    dot_general x13, matrix products, advance(): projected = jnp.dot(hidden, down_matrix, preferred_element_type=jnp.float32)  41.9 us
    dot_general x13, matrix products, advance(): jnp.dot(part_rows, gate_matrix, preferred_element_type=jnp.float32)  32.1 us
    gather x8, local copies, waits for them, and re-layouts, per_device(): recv_rows[member][gather_at]  20.7 us
    squeeze x1, local copies, waits for them, and re-layouts, per_device(): w_up[member]  17 us
    select_n x8, other arithmetic, per_device(): jnp.where(live_rows[:, None], recv_rows[member][gather_at], jnp.zeros((),...  14 us
    all_to_all x1, waiting for transfers between devices, per_device(): lax.all_to_all(send_rows, 'expert', split_axis=0, concat_axis=1, tiled=True)  9.93 us
    gather x8, local copies, waits for them, and re-layouts, per_device(): recv_scale[member][gather_at]  9.85 us
  transfers between devices with their start and end apart: 2, of which 1 were waited for; matrix products, arithmetic and copies ran while one was open for 22% of the time, Pallas kernels for 0%

commit v1 on v0

--- a/solution.py
+++ b/solution.py
@@ -7,6 +7,19 @@
 EXPERTS = 32
 TOP = 8
 CAP = 32
+
+
+def direct_the_sheets(own_rows, axis_no, original):
+    mid_arr, current_block = (own_rows.shape[:axis_no], own_rows.shape[axis_no + 1 :])
+    new = jnp.moveaxis(own_rows.reshape(*mid_arr, original, -1, *current_block), axis_no, 0)
+    return new
+
+
+def proceed_indices(t0, ndim_at):
+    side_arr = list(t0.shape[1:])
+    side_arr[ndim_at] *= t0.shape[0]
+    earlier = jnp.moveaxis(t0, 0, ndim_at).reshape(side_arr)
+    return earlier
 
 
 def lookup(values, indices, length):
@@ -130,7 +143,17 @@
             for member in range(local_experts)
         ]
     )
-    returned = lax.all_to_all(slot_results, "expert", split_axis=1, concat_axis=0, tiled=True)
+    h_now, now = (jax.lax.axis_size("expert"), jax.lax.axis_index("expert"))
+    block_now = direct_the_sheets(slot_results, 1, h_now)
+    heap = [block_now[now]]
+    for s in [*range(1, h_now)]:
+        carry_in = block_now[now ^ s]
+        heap.append(
+            jax.lax.ppermute(carry_in, "expert", perm=[(to_i, to_i ^ s) for to_i in range(h_now)])
+        )
+    wide_out = jnp.stack(heap)
+    block_now = wide_out[now ^ jnp.arange(h_now)]
+    returned = proceed_indices(block_now, 0)
     returned_flat = returned.reshape(EXPERTS * CAP, model_width)
     picked = returned_flat[targets].astype(jnp.float32).reshape(token_count, TOP, model_width)
     return jnp.sum(picked, axis=1).astype(jnp.bfloat16)

time: 298 us -> 284 us (0.953)
  blocking collectives: 49.1 us -> 0 us
  waiting for transfers between devices: 9.93 us -> 38.6 us
  starting transfers between devices: 11.4 us -> 15.9 us
  local copies, waits for them, and re-layouts: 102 us -> 106 us
  other arithmetic: 42.9 us -> 39.2 us
    all_to_all x1 -> x0, blocking collectives: 49.1 us -> none  [per_device(): lax.all_to_all(slot_results, 'expert', split_axis=1, concat_axis=0, tiled...]
    ppermute x0 -> x3, waiting for transfers between devices: none -> 29.8 us  [per_device(): jax.lax.ppermute(carry_in, 'expert', perm=[(to_i, to_i ^ s) for to_i in r...]
    unnamed x7, other arithmetic: 5.75 us -> 0.8 us
    ppermute x0 -> x3, starting transfers between devices: none -> 4.45 us  [per_device(): jax.lax.ppermute(carry_in, 'expert', perm=[(to_i, to_i ^ s) for to_i in r...]
    gather x8, local copies, waits for them, and re-layouts: 8.09 us -> 11.6 us  [spread_back(): compact_out[from_pos]]
    another operation x10 -> x9, local copies, waits for them, and re-layouts: 7.93 us -> 5.2 us
  transfers between devices with their start and end apart: 2 -> 5, of which waited for: 1 -> 3; matrix products, arithmetic and copies ran while one was open for 22% -> 23% of each run, Pallas kernels for 0% -> 0%
where the time goes in v1:
time: 284 us; the launch traced here: 280 us
  local copies, waits for them, and re-layouts  106 us (37%)
  matrix products  73.9 us (26%)
  other arithmetic  39.2 us (14%)
  waiting for transfers between devices  38.6 us (14%)
  starting transfers between devices  15.9 us (6%)
  between operations  6.01 us (2%)
    dot_general x13, matrix products, advance(): projected = jnp.dot(hidden, down_matrix, preferred_element_type=jnp.float32)  42 us
    dot_general x13, matrix products, advance(): jnp.dot(part_rows, gate_matrix, preferred_element_type=jnp.float32)  32 us
    ppermute x3, waiting for transfers between devices, per_device(): jax.lax.ppermute(carry_in, 'expert', perm=[(to_i, to_i ^ s) for to_i in r...  29.8 us
    gather x8, local copies, waits for them, and re-layouts, per_device(): recv_rows[member][gather_at]  20.7 us
    squeeze x1, local copies, waits for them, and re-layouts, per_device(): w_up[member]  17 us
    select_n x8, other arithmetic, per_device(): jnp.where(live_rows[:, None], recv_rows[member][gather_at], jnp.zeros((),...  14 us
    gather x8, local copies, waits for them, and re-layouts, spread_back(): compact_out[from_pos]  11.6 us
    gather x8, local copies, waits for them, and re-layouts, per_device(): recv_scale[member][gather_at]  9.86 us
  transfers between devices with their start and end apart: 5, of which 3 were waited for; matrix products, arithmetic and copies ran while one was open for 23% of the time, Pallas kernels for 0%

profile of v1, /device:TPU:0, one launch (start us, length us, event | category | flops | bytes accessed | tf_op | source)
XLA Modules:
  0.0 279.6 jit_solution(15443030918038372279)
XLA Ops:
  5.0 2.4 scatter_custom_fusion
  7.5 6.8 %gather_fusion = bf16[1024]{0:T(1024)(128)(2,1)S(1)} fusion(bf16[513]{0:T(1024)(128)(2,1)S(1)} %pad_maximum_fusion.1, s32[1024]{0:T(1024)S(1)} %get-tuple-element.570), kind=kCustom, calls=%fused_computation | custom fusion | bytes 8192 | tf_op jit(solution)/shard_map/gather | solution.py:105
  15.1 6.3 %all-to-all-start = ((bf16[4,2,128]{2,1,0:T(2,128)(2,1)}), bf16[4,2,128]{2,1,0:T(2,128)(2,1)S(1)}, u32[]{:S(2)}, u32[]{:S(2)}) async-start(bf16[4,2,128]{2,1,0:T(2,128)(2,1)} %reshape.1312), calls=%async_computation | async-start | bytes 4096 | tf_op jit(solution)/shard_map/all_to_all | solution.py:108
  21.4 9.6 %slice_bitcast_fusion = (bf16[768,1024]{1,0:T(8,128)(2,1)}, bf16[768,1024]{1,0:T(8,128)(2,1)}, bf16[768,1024]{1,0:T(8,128)(2,1)}, bf16[768,1024]{1,0:T(8,128)(2,...) fusion(bf16[8,768,1024]{2,1,0:T(8,128)(2,1)} %param.27), kind=kLoop, calls=%fused_computation.175 | loop fusion | bytes 25165824 | tf_op jit(solution)/shard_map/squeeze | solution.py:135
  31.0 17.0 %slice_bitcast_fusion.1 = (bf16[1024,768]{1,0:T(8,128)(2,1)S(1)}, bf16[1024,768]{1,0:T(8,128)(2,1)}, bf16[1024,768]{1,0:T(8,128)(2,1)}, bf16[1024,768]{1,0:T(8,1...) fusion(bf16[8,1024,768]{2,1,0:T(8,128)(2,1)} %param.26, ...), kind=kLoop, calls=%fused_computation.176 | loop fusion | bytes 50331648 | tf_op jit(solution)/shard_map/squeeze | solution.py:135
  48.1 5.4 %gather_fusion.2 = bf16[1024,1024]{1,0:T(8,128)(2,1)} fusion(bf16[65,1024]{1,0:T(8,128)(2,1)S(1)} %concatenate.8, s32[1024]{0:T(1024)S(1)} %get-tuple-element.569), kind=kCustom, calls=%fused_computation.2 | custom fusion | bytes 4198400 | tf_op jit(solution)/shard_map/gather | solution.py:104
  53.5 5.1 %all-to-all-start.1 = ((bf16[32,32,1024]{2,1,0:T(8,128)(2,1)}), bf16[32,32,1024]{2,1,0:T(8,128)(2,1)}, u32[]{:S(2)}, u32[]{:S(2)}) async-start(bf16[32,32,1024]{2,1,0:T(8,128)(2,1)} %bitcast.376), calls=%async_computation.1 | async-start | bytes 4194304 | tf_op jit(solution)/shard_map/all_to_all | solution.py:107
  97.5 8.9 %all-to-all-done.1 = bf16[32,32,1024]{2,1,0:T(8,128)(2,1)} async-done(((bf16[32,32,1024]{2,1,0:T(8,128)(2,1)}), bf16[32,32,1024]{2,1,0:T(8,128)(2,1)}, u32[]{:S(2)}, u32[]{:S(2)}) %all-to-all-start.1) | async-done | bytes 2097184 | tf_op jit(solution)/shard_map/all_to_all | solution.py:107
  106.4 1.8 copy.29
  109.4 2.7 gather_fusion.3
  112.2 1.8 broadcast_select_fusion.7
  114.7 12.1 %while.80 = (s32[]{:T(128)}, bf16[128,1024]{1,0:T(8,128)(2,1)}, s32[]{:T(128)}, bf16[128]{0:T(256)(128)(2,1)S(1)}, bf16[128,1024]{1,0:T(8,128)(2,1)}, /*index=5*...) while((s32[]{:T(128)}, bf16[128,1024]{1,0:T(8,128)(2,1)}, ...), condition=%wide.region_12.13_spmd, body=%wide.region_11.12_spmd.sunk | while | flops 302415936 | bytes 5506867 | solution.py:76
  114.7 2.5 fusion.291
  117.3 3.4 %fusion.292 = bf16[128,1024]{1,0:T(8,128)(2,1)} fusion(bf16[128,1024]{1,0:T(8,128)(2,1)} %get-tuple-element.1008, s32[]{:T(128)S(6)} %select_n.882, bf16[768,1024]{1,0:T(8,128)(2,1)} %get-tuple-element.1026, bf16[1024,768]{1,0:T(8,128)(2,1)} %get-tuple-element.1025, f32[64,768]{1,0:T(8,128)} %fusion.291, f32[64]{0:T(128)S(1)} %dynamic-slice_convert_fusion.16, ...), kind=kOutput, calls=%fused_computation.32.clone.1 | convolution fusion | flops 201752576 | bytes 3605760 | tf_op jit(solution)/shard_map/while/body/dot_general | solution.py:69
  120.7 2.5 fusion.291
  123.3 3.5 %fusion.292 = bf16[128,1024]{1,0:T(8,128)(2,1)} fusion(bf16[128,1024]{1,0:T(8,128)(2,1)} %get-tuple-element.1008, s32[]{:T(128)S(6)} %select_n.882, bf16[768,1024]{1,0:T(8,128)(2,1)} %get-tuple-element.1026, bf16[1024,768]{1,0:T(8,128)(2,1)} %get-tuple-element.1025, f32[64,768]{1,0:T(8,128)} %fusion.291, f32[64]{0:T(128)S(1)} %dynamic-slice_convert_fusion.16, ...), kind=kOutput, calls=%fused_computation.32.clone.1 | convolution fusion | flops 201752576 | bytes 3605760 | tf_op jit(solution)/shard_map/while/body/dot_general | solution.py:69
  126.8 2.7 gather_fusion.6
  129.5 1.7 broadcast_select_fusion.6
  132.0 6.1 %while.81 = (s32[]{:T(128)}, bf16[128,1024]{1,0:T(8,128)(2,1)}, s32[]{:T(128)}, bf16[128]{0:T(256)(128)(2,1)S(1)}, bf16[128,1024]{1,0:T(8,128)(2,1)}, /*index=5*...) while((s32[]{:T(128)}, bf16[128,1024]{1,0:T(8,128)(2,1)}, ...), condition=%wide.region_21.22_spmd, body=%wide.region_20.21_spmd.sunk | while | flops 302415936 | bytes 5506867 | solution.py:76
  132.0 2.6 fusion.298
  134.6 3.5 %fusion.299 = bf16[128,1024]{1,0:T(8,128)(2,1)} fusion(bf16[128,1024]{1,0:T(8,128)(2,1)} %get-tuple-element.1044, s32[]{:T(128)S(6)} %select_n.883, bf16[768,1024]{1,0:T(8,128)(2,1)} %get-tuple-element.1062, bf16[1024,768]{1,0:T(8,128)(2,1)} %get-tuple-element.1061, f32[64,768]{1,0:T(8,128)} %fusion.298, f32[64]{0:T(128)S(1)} %dynamic-slice_convert_fusion.17, ...), kind=kOutput, calls=%fused_computation.50.clone.1 | convolution fusion | flops 201752576 | bytes 3605760 | tf_op jit(solution)/shard_map/while/body/dot_general | solution.py:69
  138.1 2.7 gather_fusion.9
  140.8 1.8 broadcast_select_fusion.5
  143.3 6.1 %while.82 = (s32[]{:T(128)}, bf16[128,1024]{1,0:T(8,128)(2,1)}, s32[]{:T(128)}, bf16[128]{0:T(256)(128)(2,1)S(1)}, bf16[128,1024]{1,0:T(8,128)(2,1)}, /*index=5*...) while((s32[]{:T(128)}, bf16[128,1024]{1,0:T(8,128)(2,1)}, ...), condition=%wide.region_30.31_spmd, body=%wide.region_29.30_spmd.sunk | while | flops 302415936 | bytes 5506867 | solution.py:76
  143.3 2.5 fusion.305
  146.0 3.4 %fusion.306 = bf16[128,1024]{1,0:T(8,128)(2,1)} fusion(bf16[128,1024]{1,0:T(8,128)(2,1)} %get-tuple-element.1080, s32[]{:T(128)S(6)} %select_n.884, bf16[768,1024]{1,0:T(8,128)(2,1)} %get-tuple-element.1098, bf16[1024,768]{1,0:T(8,128)(2,1)} %get-tuple-element.1097, f32[64,768]{1,0:T(8,128)} %fusion.305, f32[64]{0:T(128)S(1)} %dynamic-slice_convert_fusion.18, ...), kind=kOutput, calls=%fused_computation.68.clone.1 | convolution fusion | flops 201752576 | bytes 3605760 | tf_op jit(solution)/shard_map/while/body/dot_general | solution.py:69
  149.4 2.7 gather_fusion.12
  152.2 1.8 broadcast_select_fusion.4
  154.7 12.1 %while.83 = (s32[]{:T(128)}, bf16[128,1024]{1,0:T(8,128)(2,1)}, s32[]{:T(128)}, bf16[128]{0:T(256)(128)(2,1)S(1)}, bf16[128,1024]{1,0:T(8,128)(2,1)}, /*index=5*...) while((s32[]{:T(128)}, bf16[128,1024]{1,0:T(8,128)(2,1)}, ...), condition=%wide.region_39.40_spmd, body=%wide.region_38.39_spmd.sunk | while | flops 302415936 | bytes 5506867 | solution.py:76
  154.7 2.5 fusion.312
  157.3 3.5 %fusion.313 = bf16[128,1024]{1,0:T(8,128)(2,1)} fusion(bf16[128,1024]{1,0:T(8,128)(2,1)} %get-tuple-element.1116, s32[]{:T(128)S(6)} %select_n.885, bf16[768,1024]{1,0:T(8,128)(2,1)} %get-tuple-element.1134, bf16[1024,768]{1,0:T(8,128)(2,1)} %get-tuple-element.1133, f32[64,768]{1,0:T(8,128)} %fusion.312, f32[64]{0:T(128)S(1)} %dynamic-slice_convert_fusion.19, ...), kind=kOutput, calls=%fused_computation.86.clone.1 | convolution fusion | flops 201752576 | bytes 3605760 | tf_op jit(solution)/shard_map/while/body/dot_general | solution.py:69
  160.7 2.5 fusion.312
  163.3 3.5 %fusion.313 = bf16[128,1024]{1,0:T(8,128)(2,1)} fusion(bf16[128,1024]{1,0:T(8,128)(2,1)} %get-tuple-element.1116, s32[]{:T(128)S(6)} %select_n.885, bf16[768,1024]{1,0:T(8,128)(2,1)} %get-tuple-element.1134, bf16[1024,768]{1,0:T(8,128)(2,1)} %get-tuple-element.1133, f32[64,768]{1,0:T(8,128)} %fusion.312, f32[64]{0:T(128)S(1)} %dynamic-slice_convert_fusion.19, ...), kind=kOutput, calls=%fused_computation.86.clone.1 | convolution fusion | flops 201752576 | bytes 3605760 | tf_op jit(solution)/shard_map/while/body/dot_general | solution.py:69
  166.8 2.7 gather_fusion.15
  169.5 1.8 broadcast_select_fusion.3
  172.0 6.1 %while.84 = (s32[]{:T(128)}, bf16[128,1024]{1,0:T(8,128)(2,1)}, s32[]{:T(128)}, bf16[128]{0:T(256)(128)(2,1)S(1)}, bf16[128,1024]{1,0:T(8,128)(2,1)}, /*index=5*...) while((s32[]{:T(128)}, bf16[128,1024]{1,0:T(8,128)(2,1)}, ...), condition=%wide.region_48.49_spmd, body=%wide.region_47.48_spmd.sunk | while | flops 302415936 | bytes 5506867 | solution.py:76
  172.0 2.5 fusion.319
  174.7 3.5 %fusion.320 = bf16[128,1024]{1,0:T(8,128)(2,1)} fusion(bf16[128,1024]{1,0:T(8,128)(2,1)} %get-tuple-element.1152, s32[]{:T(128)S(6)} %select_n.886, bf16[768,1024]{1,0:T(8,128)(2,1)} %get-tuple-element.1170, bf16[1024,768]{1,0:T(8,128)(2,1)} %get-tuple-element.1169, f32[64,768]{1,0:T(8,128)} %fusion.319, f32[64]{0:T(128)S(1)} %dynamic-slice_convert_fusion.20, ...), kind=kOutput, calls=%fused_computation.104.clone.1 | convolution fusion | flops 201752576 | bytes 3605760 | tf_op jit(solution)/shard_map/while/body/dot_general | solution.py:69
  178.1 2.7 gather_fusion.18
  180.8 1.7 broadcast_select_fusion.2
  183.3 12.2 %while.85 = (s32[]{:T(128)}, bf16[128,1024]{1,0:T(8,128)(2,1)}, s32[]{:T(128)}, bf16[128]{0:T(256)(128)(2,1)S(1)}, bf16[128,1024]{1,0:T(8,128)(2,1)}, /*index=5*...) while((s32[]{:T(128)}, bf16[128,1024]{1,0:T(8,128)(2,1)}, ...), condition=%wide.region_57.58_spmd, body=%wide.region_56.57_spmd.sunk | while | flops 302415936 | bytes 5506867 | solution.py:76
  183.3 2.6 fusion.326
  186.0 3.4 %fusion.327 = bf16[128,1024]{1,0:T(8,128)(2,1)} fusion(bf16[128,1024]{1,0:T(8,128)(2,1)} %get-tuple-element.1188, s32[]{:T(128)S(6)} %select_n.887, bf16[768,1024]{1,0:T(8,128)(2,1)} %get-tuple-element.1206, bf16[1024,768]{1,0:T(8,128)(2,1)} %get-tuple-element.1205, f32[64,768]{1,0:T(8,128)} %fusion.326, f32[64]{0:T(128)S(1)} %dynamic-slice_convert_fusion.21, ...), kind=kOutput, calls=%fused_computation.122.clone.1 | convolution fusion | flops 201752576 | bytes 3605760 | tf_op jit(solution)/shard_map/while/body/dot_general | solution.py:69
  189.4 2.6 fusion.326
  192.0 3.5 %fusion.327 = bf16[128,1024]{1,0:T(8,128)(2,1)} fusion(bf16[128,1024]{1,0:T(8,128)(2,1)} %get-tuple-element.1188, s32[]{:T(128)S(6)} %select_n.887, bf16[768,1024]{1,0:T(8,128)(2,1)} %get-tuple-element.1206, bf16[1024,768]{1,0:T(8,128)(2,1)} %get-tuple-element.1205, f32[64,768]{1,0:T(8,128)} %fusion.326, f32[64]{0:T(128)S(1)} %dynamic-slice_convert_fusion.21, ...), kind=kOutput, calls=%fused_computation.122.clone.1 | convolution fusion | flops 201752576 | bytes 3605760 | tf_op jit(solution)/shard_map/while/body/dot_general | solution.py:69
  195.5 2.7 gather_fusion.21
  198.2 1.7 broadcast_select_fusion.1
  200.7 11.3 %while.86 = (s32[]{:T(128)}, bf16[128,1024]{1,0:T(8,128)(2,1)}, s32[]{:T(128)}, bf16[128]{0:T(256)(128)(2,1)S(1)}, bf16[128,1024]{1,0:T(8,128)(2,1)}, /*index=5*...) while((s32[]{:T(128)}, bf16[128,1024]{1,0:T(8,128)(2,1)}, ...), condition=%wide.region_66.67_spmd, body=%wide.region_65.66_spmd.sunk | while | flops 302415936 | bytes 5506867 | solution.py:76
  200.7 2.5 fusion.333
  203.3 3.0 %fusion.334 = bf16[128,1024]{1,0:T(8,128)(2,1)} fusion(bf16[128,1024]{1,0:T(8,128)(2,1)} %get-tuple-element.1224, s32[]{:T(128)S(6)} %select_n.888, bf16[768,1024]{1,0:T(8,128)(2,1)} %get-tuple-element.1242, bf16[1024,768]{1,0:T(8,128)(2,1)S(1)} %get-tuple-element.1241, f32[64,768]{1,0:T(8,128)} %fusion.333, ...), kind=kOutput, calls=%fused_computation.140.clone.1 | convolution fusion | flops 201752576 | bytes 3605760 | tf_op jit(solution)/shard_map/while/body/dot_general | solution.py:69
  206.3 2.5 fusion.333
  209.0 3.1 %fusion.334 = bf16[128,1024]{1,0:T(8,128)(2,1)} fusion(bf16[128,1024]{1,0:T(8,128)(2,1)} %get-tuple-element.1224, s32[]{:T(128)S(6)} %select_n.888, bf16[768,1024]{1,0:T(8,128)(2,1)} %get-tuple-element.1242, bf16[1024,768]{1,0:T(8,128)(2,1)S(1)} %get-tuple-element.1241, f32[64,768]{1,0:T(8,128)} %fusion.333, ...), kind=kOutput, calls=%fused_computation.140.clone.1 | convolution fusion | flops 201752576 | bytes 3605760 | tf_op jit(solution)/shard_map/while/body/dot_general | solution.py:69
  213.6 1.7 broadcast_select_fusion
  215.3 9.2 %while.87 = (s32[]{:T(128)}, bf16[128,1024]{1,0:T(8,128)(2,1)S(1)}, s32[]{:T(128)}, bf16[128]{0:T(256)(128)(2,1)S(1)}, bf16[128,1024]{1,0:T(8,128)(2,1)}, /*inde...) while((s32[]{:T(128)}, bf16[128,1024]{1,0:T(8,128)(2,1)S(1)}, ...), condition=%wide.region_75.76_spmd, body=%wide.region_74.75_spmd.sunk | while | flops 302415936 | bytes 5507123 | solution.py:76
  215.4 2.0 fusion.340
  217.4 2.4 fusion.341
  219.9 2.0 fusion.340
  221.9 2.4 fusion.341
  224.6 2.1 gather_fusion.4
  239.5 3.0 %collective-permute-start = (bf16[8,32,1024]{2,1,0:T(8,128)(2,1)S(1)}, bf16[8,32,1024]{2,1,0:T(8,128)(2,1)S(1)}, u32[]{:S(2)}, u32[]{:S(2)}) collective-permute-start(bf16[8,32,1024]{2,1,0:T(8,128)(2,1)S(1)} %get-tuple-element.560), channel_id=1, source_target_pairs={{0,4},{4,0},{8,12},{12,8},{1,5},{5,1},{9,13},{13,9},{2,6},{6,2},{1... | collective-permute-start | bytes 1572872 | tf_op jit(solution)/shard_map/ppermute | solution.py:152
  242.5 12.2 %collective-permute-done.2 = bf16[8,32,1024]{2,1,0:T(8,128)(2,1)S(1)} collective-permute-done((bf16[8,32,1024]{2,1,0:T(8,128)(2,1)S(1)}, bf16[8,32,1024]{2,1,0:T(8,128)(2,1)S(1)}, u32[]{:S(2)}, u32[]{:S(2)}) %collective-permute-start.2) | collective-permute-done | bytes 524320 | tf_op jit(solution)/shard_map/ppermute | solution.py:152
  254.7 17.5 %collective-permute-done.1 = bf16[8,32,1024]{2,1,0:T(8,128)(2,1)S(1)} collective-permute-done((bf16[8,32,1024]{2,1,0:T(8,128)(2,1)S(1)}, bf16[8,32,1024]{2,1,0:T(8,128)(2,1)S(1)}, u32[]{:S(2)}, u32[]{:S(2)}) %collective-permute-start.1) | collective-permute-done | bytes 524320 | tf_op jit(solution)/shard_map/ppermute | solution.py:152
  273.9 2.3 gather_fusion.26
  276.1 2.1 gather_fusion.27
  (225 shorter events, 63.7 us)
Async XLA Ops:
  15.1 38.5 %all-to-all-start = ((bf16[4,2,128]{2,1,0:T(2,128)(2,1)}), bf16[4,2,128]{2,1,0:T(2,128)(2,1)S(1)}, u32[]{:S(2)}, u32[]{:S(2)}) async-start(bf16[4,2,128]{2,1,0:T(2,128)(2,1)} %reshape.1312), calls=%async_computation | async-start | bytes 4096 | tf_op jit(solution)/shard_map/all_to_all | solution.py:108
  31.0 17.1 %copy-start.12 = (bf16[64,1024]{1,0:T(8,128)(2,1)S(1)}, bf16[64,1024]{1,0:T(8,128)(2,1)}, u32[]{:S(2)}) copy-start(bf16[64,1024]{1,0:T(8,128)(2,1)} %param.22) | copy-start | bytes 393220
  53.5 52.8 %all-to-all-start.1 = ((bf16[32,32,1024]{2,1,0:T(8,128)(2,1)}), bf16[32,32,1024]{2,1,0:T(8,128)(2,1)}, u32[]{:S(2)}, u32[]{:S(2)}) async-start(bf16[32,32,1024]{2,1,0:T(8,128)(2,1)} %bitcast.376), calls=%async_computation.1 | async-start | bytes 4194304 | tf_op jit(solution)/shard_map/all_to_all | solution.py:107
  138.1 5.2 %copy-start.17 = (bf16[128]{0:T(256)(128)(2,1)S(1)}, bf16[128]{0:T(256)(128)(2,1)}, u32[]{:S(2)}) copy-start(bf16[128]{0:T(256)(128)(2,1)} %broadcast_select_fusion.13) | copy-start | bytes 772
  149.4 5.2 %copy-start.16 = (bf16[128]{0:T(256)(128)(2,1)S(1)}, bf16[128]{0:T(256)(128)(2,1)}, u32[]{:S(2)}) copy-start(bf16[128]{0:T(256)(128)(2,1)} %broadcast_select_fusion.12) | copy-start | bytes 772
  166.8 5.2 %copy-start.15 = (bf16[128]{0:T(256)(128)(2,1)S(1)}, bf16[128]{0:T(256)(128)(2,1)}, u32[]{:S(2)}) copy-start(bf16[128]{0:T(256)(128)(2,1)} %broadcast_select_fusion.11) | copy-start | bytes 772
  178.1 5.2 %copy-start.14 = (bf16[128]{0:T(256)(128)(2,1)S(1)}, bf16[128]{0:T(256)(128)(2,1)}, u32[]{:S(2)}) copy-start(bf16[128]{0:T(256)(128)(2,1)} %broadcast_select_fusion.10) | copy-start | bytes 772
  195.5 5.2 %copy-start.13 = (bf16[128]{0:T(256)(128)(2,1)S(1)}, bf16[128]{0:T(256)(128)(2,1)}, u32[]{:S(2)}) copy-start(bf16[128]{0:T(256)(128)(2,1)} %broadcast_select_fusion.9) | copy-start | bytes 772
  212.0 3.3 %copy-start = (bf16[1024,768]{1,0:T(8,128)(2,1)S(1)}, bf16[1024,768]{1,0:T(8,128)(2,1)}, u32[]{:S(2)}) copy-start(bf16[1024,768]{1,0:T(8,128)(2,1)} %get-tuple-element.1252) | copy-start | bytes 4718596
  224.5 2.2 copy-start.1
  226.6 1.0 copy-start.2
  227.6 1.0 copy-start.3
  228.5 1.6 copy-start.4
  230.1 1.6 copy-start.5
  231.7 1.6 copy-start.6
  234.8 1.8 copy-start.7
  234.8 2.0 copy-start.8
  236.4 0.9 copy-start.9
  236.4 1.1 copy-start.10
  236.4 1.2 copy-start.11
  238.0 16.7 %collective-permute-start.2 = (bf16[8,32,1024]{2,1,0:T(8,128)(2,1)S(1)}, bf16[8,32,1024]{2,1,0:T(8,128)(2,1)S(1)}, u32[]{:S(2)}, u32[]{:S(2)}) collective-permute-start(bf16[8,32,1024]{2,1,0:T(8,128)(2,1)S(1)} %get-tuple-element.558), channel_id=1, source_target_pairs={{0,12},{4,8},{8,4},{12,0},{1,13},{5,9},{9,5},{13,1},{2,14},{6,10},... | collective-permute-start | bytes 1572872 | tf_op jit(solution)/shard_map/ppermute | solution.py:152
  239.5 32.7 %collective-permute-start.1 = (bf16[8,32,1024]{2,1,0:T(8,128)(2,1)S(1)}, bf16[8,32,1024]{2,1,0:T(8,128)(2,1)S(1)}, u32[]{:S(2)}, u32[]{:S(2)}) collective-permute-start(bf16[8,32,1024]{2,1,0:T(8,128)(2,1)S(1)} %get-tuple-element.559), channel_id=1, source_target_pairs={{0,8},{4,12},{8,0},{12,4},{1,9},{5,13},{9,1},{13,5},{2,10},{6,14},... | collective-permute-start | bytes 1572872 | tf_op jit(solution)/shard_map/ppermute | solution.py:152
  239.5 32.7 %collective-permute-start = (bf16[8,32,1024]{2,1,0:T(8,128)(2,1)S(1)}, bf16[8,32,1024]{2,1,0:T(8,128)(2,1)S(1)}, u32[]{:S(2)}, u32[]{:S(2)}) collective-permute-start(bf16[8,32,1024]{2,1,0:T(8,128)(2,1)S(1)} %get-tuple-element.560), channel_id=1, source_target_pairs={{0,4},{4,0},{8,12},{12,8},{1,5},{5,1},{9,13},{13,9},{2,6},{6,2},{1... | collective-permute-start | bytes 1572872 | tf_op jit(solution)/shard_map/ppermute | solution.py:152
